TPU v7x, 32 devices: a whole 2x2x4 slice. The times are simulated.
32 devices in a mesh: sim: 8 (over y, x, core), ana: 4 (over z).
Axes of the slice: x: 2, y: 2, z: 4, core: 2. Of those that a mesh axis runs over, the one named last changes fastest.
Arguments:
- initial_disp: float32 [256, 512, 128], P('ana', 'sim'), may hold values from -24 to 24
- initial_vel: float32 [256, 512, 128], P('ana', 'sim'), may hold values from -2 to 2
- stiffness: float32 [512, 128], P('sim'), may hold values from 0.05 to 0.35
- basis: float32 [512, 128, 512], P(('sim', 'ana')), may hold values from -5 to 5
- rotation: float32 [768, 512], replicated, may hold values from -0.21875 to 0.21875
Outputs:
- basis_out: float32 [512, 128, 512], P(('sim', 'ana'))
- coords: float32 [512, 256], replicated
All inputs are finite; a program needn't handle non-finite values.
Results may differ from a plain program's by a relative error of at most 0.000054.
Values sent between devices are 32-bit elements; how exact they have to be, the bound alone decides.
No kernel may reach another device: no remote copies, remote signals or barrier semaphores. Data moves between devices by JAX's collectives and lax.ppermute only.
A program may use at most 64 MiB of HBM per device.

v0:
```python
import math
import jax
import jax.numpy as jnp
from jax import lax
from jax.sharding import PartitionSpec as P

M = 256
K = 512
STEPS = 4
epsilon = 1e-06


def with_halo(value, sides, width):
    for axis, dim in sides:
        size, length = (lax.axis_size(axis), value.shape[dim])
        up = [(i, (i + 1) % size) for i in range(size - 1)]
        down = [(j, i) for i, j in up]
        last = lax.slice_in_dim(value, length - width, length, axis=dim)
        initial = lax.slice_in_dim(value, 0, width, axis=dim)
        before = lax.ppermute(last, axis, up)
        after = lax.ppermute(initial, axis, down)
        value = jnp.concatenate([before, value, after], axis=dim)
    return value


def accelerate(displace, stiffness):
    padded = with_halo(displace, (("sim", 1),), 1)
    padded = jnp.pad(padded, ((0, 0), (0, 0), (1, 1)))
    laplace = (
        padded[:, 2:, 1:-1]
        + padded[:, :-2, 1:-1]
        + padded[:, 1:-1, 2:]
        + padded[:, 1:-1, :-2]
        - 4.0 * displace
    )
    return stiffness[None] * (
        laplace - 0.5 * displace * displace * displace / (1.0 + displace * displace)
    )


def contract(left, right, left_dim, right_dim):
    return lax.dot_general(
        left,
        right,
        (((left_dim,), (right_dim,)), ((), ())),
        precision=lax.Precision.HIGHEST,
        preferred_element_type=jnp.float32,
    )


def per_device(initial_disp, initial_vel, stiffness, basis, rotation):
    displace = initial_disp
    velocity = initial_vel
    for step_index in range(STEPS):
        velocity = velocity + accelerate(displace, stiffness)
        displace = displace + velocity
    row_count = basis.shape[0] * basis.shape[1] * lax.axis_size("sim") * lax.axis_size("ana")
    basis_rows = basis.reshape(-1, K)
    totals = lax.psum(jnp.sum(displace * displace, axis=(1, 2)), "sim")
    member_scale = jnp.sqrt(totals / row_count + epsilon)
    outgoing = displace / member_scale[:, None, None]
    arrived = lax.all_to_all(outgoing, "ana", split_axis=1, concat_axis=0, tiled=True)
    unscaled = arrived.reshape(M, -1)
    coefficients = lax.psum(contract(basis_rows, unscaled, 0, 1), ("sim", "ana")) / row_count
    remainder = unscaled - contract(coefficients, basis_rows, 0, 1)
    gram_matrix = lax.psum(contract(remainder, remainder, 1, 1), ("sim", "ana")) / row_count
    factor = jnp.linalg.cholesky(gram_matrix)
    fresh_basis = jax.scipy.linalg.solve_triangular(factor, remainder, lower=True)
    top_rows = rotation[:K]
    bottom_rows = rotation[K:]
    basis_out = contract(basis_rows, top_rows, 1, 0) + contract(fresh_basis, bottom_rows, 0, 0)
    coords = (
        contract(top_rows, coefficients, 0, 0) + contract(bottom_rows, factor, 0, 1)
    ) * math.sqrt(K)
    return (basis_out.reshape(basis.shape), coords)


def solution(mesh):
    in_specs = (
        P("ana", "sim", None),
        P("ana", "sim", None),
        P("sim", None),
        P(("sim", "ana"), None, None),
        P(),
    )
    out_specs = (P(("sim", "ana"), None, None), P())
    return jax.shard_map(
        per_device, mesh=mesh, in_specs=in_specs, out_specs=out_specs, check_vma=False
    )
```

profile of v0, /device:TPU:0, one launch (start us, length us, event | category | flops | bytes accessed | tf_op | source)
XLA Modules:
  0.0 476.9 jit_solution(9723111592130537525)
XLA Ops:
  7.2 2.8 copy.23
  10.0 1.3 collective-permute-start
  11.4 3.3 collective-permute-start.1
  14.7 0.8 collective-permute-done.1
  15.5 1.2 select_maximum_fusion.6
  16.7 5.5 %copy_add_fusion = (f32[64,64,128]{2,0,1:T(8,128)S(1)}, f32[64,64,128]{2,0,1:T(8,128)S(1)}) fusion(f32[64,64,128]{2,1,0:T(8,128)S(1)} %copy-done.3, f32[64,64,128]{2,0,1:T(8,128)S(1)} %copy.23, f32[64,66,130]{2,0,1:T(8,128)S(1)} %select_maximum_fusion.6, f32[64,1,128]{2,0,1:T(8,128)S(1)} %collective-permute-done.1, ...), kind=kLoop, calls=%fused_computation.118 | loop fusion | flops 8912896 | bytes 14778368 | tf_op jit(solution)/shard_map/add | solution.py:56
  22.2 1.3 collective-permute-start.2
  23.5 5.3 %collective-permute-start.3 = (f32[64,1,128]{2,0,1:T(8,128)S(1)}, f32[64,1,128]{2,0,1:T(8,128)S(1)}, u32[]{:S(2)}, u32[]{:S(2)}) collective-permute-start(f32[64,1,128]{2,0,1:T(8,128)S(1)} %get-tuple-element.36), channel_id=1, source_target_pairs={{0,4},{4,8},{8,12},{12,16},{16,20},{20,24},{24,28},{1,5},{5,9},{9,... | collective-permute-start | bytes 98312 | tf_op jit(solution)/shard_map/ppermute | solution.py:20
  28.8 0.8 collective-permute-done.3
  29.6 1.2 select_maximum_fusion.4
  30.8 1.9 fusion.67
  32.7 1.3 collective-permute-start.4
  34.0 5.0 %collective-permute-start.5 = (f32[64,1,128]{2,0,1:T(8,128)S(1)}, f32[64,1,128]{2,0,1:T(8,128)S(1)}, u32[]{:S(2)}, u32[]{:S(2)}) collective-permute-start(f32[64,1,128]{2,0,1:T(8,128)S(1)} %get-tuple-element.34), channel_id=1, source_target_pairs={{0,4},{4,8},{8,12},{12,16},{16,20},{20,24},{24,28},{1,5},{5,9},{9,... | collective-permute-start | bytes 98312 | tf_op jit(solution)/shard_map/ppermute | solution.py:20
  39.1 0.8 collective-permute-done.5
  39.9 1.2 select_maximum_fusion.2
  41.1 1.8 fusion.65
  42.9 1.3 collective-permute-start.6
  44.2 5.0 %collective-permute-start.7 = (f32[64,1,128]{2,0,1:T(8,128)S(1)}, f32[64,1,128]{2,0,1:T(8,128)S(1)}, u32[]{:S(2)}, u32[]{:S(2)}) collective-permute-start(f32[64,1,128]{2,0,1:T(8,128)S(1)} %get-tuple-element.32), channel_id=1, source_target_pairs={{0,4},{4,8},{8,12},{12,16},{16,20},{20,24},{24,28},{1,5},{5,9},{9,... | collective-permute-start | bytes 98312 | tf_op jit(solution)/shard_map/ppermute | solution.py:20
  49.3 0.8 collective-permute-done.7
  50.1 1.2 select_maximum_fusion
  51.3 2.0 multiply_reduce_fusion
  53.3 17.1 %psum.21 = f32[64]{0:T(128)S(1)} all-reduce(f32[64]{0:T(128)S(1)} %get-tuple-element.22), channel_id=1, replica_groups=mesh['sim'=8,'ana'=4] {'sim'}, use_global_device_ids=true, to_apply=%region_1.2 | all-reduce | flops 64 | bytes 512 | tf_op jit(solution)/shard_map/psum | solution.py:59
  70.7 53.3 %all_to_all.15 = f32[64,64,128]{2,0,1:T(8,128)S(1)} all-to-all(f32[64,64,128]{2,0,1:T(8,128)S(1)} %broadcast_divide_fusion), channel_id=1, replica_groups=mesh['sim'=8,'ana'=4] {'ana'}, dimensions={1} | all-to-all | bytes 4194304 | tf_op jit(solution)/shard_map/all_to_all | solution.py:62
  124.0 1.2 copy.24
  125.3 1.3 copy-done.2
  126.6 4.9 %fusion.34 = f32[512,256]{0,1:T(8,128)} fusion(f32[2048,512]{1,0:T(8,128)S(1)} %bitcast.54, f32[32,8,16,128]{3,2,1,0:T(8,128)S(1)} %bitcast.55), kind=kOutput, calls=%fused_computation.71 | convolution fusion | flops 3221225472 | bytes 6815744 | tf_op jit(solution)/shard_map/dot_general | solution.py:42
  131.5 128.3 %all-reduce.8.cloned.1.call-done = f32[512,256]{0,1:T(8,128)} async-done(((f32[512,256]{0,1:T(8,128)}), f32[512,256]{0,1:T(8,128)}) %all-reduce.8.cloned.1.call-update) | async-done | bytes 524304 | tf_op jit(solution)/shard_map/psum | solution.py:64
  259.9 7.1 %convolution_subtract_fusion = f32[256,2048]{1,0:T(8,128)S(1)} fusion(f32[2048,512]{1,0:T(8,128)} %bitcast.52, f32[32,8,16,128]{3,2,1,0:T(8,128)} %bitcast.56, f32[512,256]{0,1:T(8,128)} %all-reduce.8.cloned.1.call-done), kind=kOutput, calls=%fused_computation.18 | convolution fusion | flops 3221880832 | bytes 8912896 | tf_op jit(solution)/shard_map/dot_general | solution.py:42
  267.0 2.6 fusion.75
  269.6 10.3 %fusion.40 = f32[2048,512]{1,0:T(8,128)} fusion(f32[2048,512]{1,0:T(8,128)} %bitcast.53, f32[768,512]{1,0:T(8,128)} %param.9), kind=kOutput, calls=%fused_computation.77 | convolution fusion | flops 6442450944 | bytes 9437184 | tf_op jit(solution)/shard_map/dot_general | solution.py:42
  279.9 113.8 %all-reduce.10.cloned.1.call-done = f32[256,256]{0,1:T(8,128)} async-done(((f32[256,256]{0,1:T(8,128)}), f32[256,256]{0,1:T(8,128)}) %all-reduce.10.cloned.1.call-update) | async-done | bytes 262160 | tf_op jit(solution)/shard_map/psum | solution.py:66
  393.6 1.0 broadcast_multiply_fusion
  394.8 1.0 fusion.47
  395.8 11.7 %cholesky.50 = f32[128,128]{1,0:T(8,128)S(1)} custom-call(f32[128,128]{1,0:T(8,128)S(1)} %cholesky.118), custom_call_target="Cholesky" | custom-call | tf_op jit(solution)/shard_map/jit(cholesky)/cholesky | solution.py:67
  407.6 9.8 %custom-call.15 = f32[1,128,128]{1,2,0:T(8,128)S(1)} custom-call(f32[1,128,128]{2,1,0:T(8,128)S(1)} %get-tuple-element.43), custom_call_target="InvertDiagBlocksLowerTriangular" | custom-call | tf_op jit(solution)/shard_map/jit(cholesky)/cholesky | solution.py:67
  417.9 11.7 %cholesky.105 = f32[128,128]{1,0:T(8,128)S(1)} custom-call(f32[128,128]{1,0:T(8,128)S(1)} %convolution_subtract_fusion.2), custom_call_target="Cholesky" | custom-call | tf_op jit(solution)/shard_map/jit(cholesky)/cholesky | solution.py:67
  431.7 1.8 fusion.42
  433.5 0.7 fusion.50
  434.2 1.1 fusion.33
  435.3 1.0 copy.27
  436.3 4.0 while.1
  437.2 1.3 bitcast_dynamic-update-slice_fusion.2
  439.1 1.3 bitcast_dynamic-update-slice_fusion.2
  440.4 19.7 %custom-call.16 = f32[2,128,128]{1,2,0:T(8,128)S(1)} custom-call(f32[2,128,128]{2,1,0:T(8,128)S(1)} %get-tuple-element.9), custom_call_target="InvertDiagBlocksLowerTriangular" | custom-call | tf_op jit(solution)/shard_map/jit(_solve_triangular)/triangular_solve | solution.py:68
  460.1 1.1 fusion.37
  461.1 1.0 convolution_subtract_fusion.1
  462.2 1.0 fusion.55
  463.3 6.3 %convolution_add_fusion = f32[2048,512]{1,0:T(8,128)} fusion(f32[2048,512]{1,0:T(8,128)S(1)} %copy-done.1, f32[128,2048]{1,0:T(8,128)S(1)} %fusion.55, f32[128,2048]{1,0:T(8,128)S(1)} %fusion.37, f32[768,512]{1,0:T(8,128)} %param.9), kind=kOutput, calls=%fused_computation.13 | convolution fusion | flops 3222798336 | bytes 11010048 | tf_op jit(solution)/shard_map/dot_general | solution.py:42
  (46 shorter events, 3.3 us)
Async XLA Ops:
  7.2 252.7 %all-reduce.8.cloned.1.call-start = ((), (), s32[]{:S(2)}) async-start(), calls=%async_computation.1 | async-start | bytes 1048576 | tf_op jit(solution)/shard_map/psum | solution.py:64
  10.0 4.6 collective-permute-start
  11.3 5.4 %copy-start.3 = (f32[64,64,128]{2,1,0:T(8,128)S(1)}, f32[64,64,128]{2,1,0:T(8,128)}, u32[]{:S(2)}) copy-start(f32[64,64,128]{2,1,0:T(8,128)} %param.5) | copy-start | bytes 6291460
  11.3 5.4 %copy-start.5 = (f32[64,64,128]{2,1,0:T(8,128)S(1)}, f32[64,64,128]{2,1,0:T(8,128)}, u32[]{:S(2)}) copy-start(f32[64,64,128]{2,1,0:T(8,128)} %param.6) | copy-start | bytes 6291460
  11.4 5.4 %copy-start.8 = (f32[64,128]{1,0:T(8,128)S(1)}, f32[64,128]{1,0:T(8,128)}, u32[]{:S(2)}) copy-start(f32[64,128]{1,0:T(8,128)} %param.7) | copy-start | bytes 98308
  11.4 4.1 collective-permute-start.1
  22.2 6.6 %collective-permute-start.2 = (f32[64,1,128]{2,0,1:T(8,128)S(1)}, f32[64,1,128]{2,0,1:T(8,128)S(1)}, u32[]{:S(2)}, u32[]{:S(2)}) collective-permute-start(f32[64,1,128]{2,0,1:T(8,128)S(1)} %get-tuple-element.37), channel_id=1, source_target_pairs={{4,0},{8,4},{12,8},{16,12},{20,16},{24,20},{28,24},{5,1},{9,5},{13... | collective-permute-start | bytes 98312 | tf_op jit(solution)/shard_map/ppermute | solution.py:21
  23.5 6.1 %collective-permute-start.3 = (f32[64,1,128]{2,0,1:T(8,128)S(1)}, f32[64,1,128]{2,0,1:T(8,128)S(1)}, u32[]{:S(2)}, u32[]{:S(2)}) collective-permute-start(f32[64,1,128]{2,0,1:T(8,128)S(1)} %get-tuple-element.36), channel_id=1, source_target_pairs={{0,4},{4,8},{8,12},{12,16},{16,20},{20,24},{24,28},{1,5},{5,9},{9,... | collective-permute-start | bytes 98312 | tf_op jit(solution)/shard_map/ppermute | solution.py:20
  32.7 6.3 %collective-permute-start.4 = (f32[64,1,128]{2,0,1:T(8,128)S(1)}, f32[64,1,128]{2,0,1:T(8,128)S(1)}, u32[]{:S(2)}, u32[]{:S(2)}) collective-permute-start(f32[64,1,128]{2,0,1:T(8,128)S(1)} %get-tuple-element.35), channel_id=1, source_target_pairs={{4,0},{8,4},{12,8},{16,12},{20,16},{24,20},{28,24},{5,1},{9,5},{13... | collective-permute-start | bytes 98312 | tf_op jit(solution)/shard_map/ppermute | solution.py:21
  34.0 5.9 %collective-permute-start.5 = (f32[64,1,128]{2,0,1:T(8,128)S(1)}, f32[64,1,128]{2,0,1:T(8,128)S(1)}, u32[]{:S(2)}, u32[]{:S(2)}) collective-permute-start(f32[64,1,128]{2,0,1:T(8,128)S(1)} %get-tuple-element.34), channel_id=1, source_target_pairs={{0,4},{4,8},{8,12},{12,16},{16,20},{20,24},{24,28},{1,5},{5,9},{9,... | collective-permute-start | bytes 98312 | tf_op jit(solution)/shard_map/ppermute | solution.py:20
  42.9 6.3 %collective-permute-start.6 = (f32[64,1,128]{2,0,1:T(8,128)S(1)}, f32[64,1,128]{2,0,1:T(8,128)S(1)}, u32[]{:S(2)}, u32[]{:S(2)}) collective-permute-start(f32[64,1,128]{2,0,1:T(8,128)S(1)} %get-tuple-element.33), channel_id=1, source_target_pairs={{4,0},{8,4},{12,8},{16,12},{20,16},{24,20},{28,24},{5,1},{9,5},{13... | collective-permute-start | bytes 98312 | tf_op jit(solution)/shard_map/ppermute | solution.py:21
  44.2 5.9 %collective-permute-start.7 = (f32[64,1,128]{2,0,1:T(8,128)S(1)}, f32[64,1,128]{2,0,1:T(8,128)S(1)}, u32[]{:S(2)}, u32[]{:S(2)}) collective-permute-start(f32[64,1,128]{2,0,1:T(8,128)S(1)} %get-tuple-element.32), channel_id=1, source_target_pairs={{0,4},{4,8},{8,12},{12,16},{16,20},{20,24},{24,28},{1,5},{5,9},{9,... | collective-permute-start | bytes 98312 | tf_op jit(solution)/shard_map/ppermute | solution.py:20
  124.0 2.5 copy-start
  125.3 1.3 copy-start.2
  131.5 262.1 %all-reduce.10.cloned.1.call-start = ((), (), s32[]{:S(2)}) async-start(), calls=%async_computation.2 | async-start | bytes 524288 | tf_op jit(solution)/shard_map/psum | solution.py:66
  394.6 39.6 %copy-start.6 = (f32[512,256]{0,1:T(8,128)S(1)}, f32[512,256]{0,1:T(8,128)}, u32[]{:S(2)}) copy-start(f32[512,256]{0,1:T(8,128)} %all-reduce.8.cloned.1.call-done) | copy-start | bytes 1572868
  431.6 2.6 copy-start.4
  434.2 2.1 copy-start.7
  461.1 2.2 copy-start.1
Sparse Core Ops, SparseCore 0:
  131.6 128.2 all-reduce.7
  269.7 123.9 all-reduce.9
where the time goes:
time: 486 us; the launch traced here: 477 us
  waiting for transfers between devices  245 us (50%)
  other arithmetic  72.6 us (15%)
  blocking collectives  70.4 us (14%)
  matrix products  37.5 us (8%)
  starting transfers between devices  23.8 us (5%)
  between operations  16.2 us (3%)
  local copies, waits for them, and re-layouts  10.5 us (2%)
    psum x1, waiting for transfers between devices, per_device(): lax.psum(contract(basis_rows, unscaled, 0, 1), ('sim', 'ana')) / row_count  128 us
    psum x1, waiting for transfers between devices, per_device(): lax.psum(contract(remainder, remainder, 1, 1), ('sim', 'ana')) / row_count  114 us
    all_to_all x1, blocking collectives, per_device(): lax.all_to_all(outgoing, 'ana', split_axis=1, concat_axis=0, tiled=True)  53.3 us
    another operation x6, other arithmetic, per_device(): factor = jnp.linalg.cholesky(gram_matrix)  34 us
    dot_general x7, matrix products, contract(): lax.dot_general(left, right, (((left_dim,), (right_dim,)), ((), ())), pre...  33.9 us
    another operation x3, other arithmetic, per_device(): jax.scipy.linalg.solve_triangular(factor, remainder, lower=True)  20.4 us
    ppermute x4, starting transfers between devices, with_halo(): before = lax.ppermute(last, axis, up)  18.6 us
    psum x1, blocking collectives, per_device(): totals = lax.psum(jnp.sum(displace * displace, axis=(1, 2)), 'sim')  17.1 us
  transfers between devices with their start and end apart: 10, of which 6 were waited for; matrix products, arithmetic and copies ran while one was open for 2% of the time, Pallas kernels for 0%

commit v1 on v0

--- a/solution.py
+++ b/solution.py
@@ -8,6 +8,11 @@
 K = 512
 STEPS = 4
 epsilon = 1e-06
+
+
+def one_after_other(array, first, second):
+    inner = lax.psum(array, first)
+    return lax.psum(inner, second)
 
 
 def with_halo(value, sides, width):
@@ -63,7 +68,7 @@
     unscaled = arrived.reshape(M, -1)
     coefficients = lax.psum(contract(basis_rows, unscaled, 0, 1), ("sim", "ana")) / row_count
     remainder = unscaled - contract(coefficients, basis_rows, 0, 1)
-    gram_matrix = lax.psum(contract(remainder, remainder, 1, 1), ("sim", "ana")) / row_count
+    gram_matrix = one_after_other(contract(remainder, remainder, 1, 1), "ana", "sim") / row_count
     factor = jnp.linalg.cholesky(gram_matrix)
     fresh_basis = jax.scipy.linalg.solve_triangular(factor, remainder, lower=True)
     top_rows = rotation[:K]

time: 486 us -> 455 us (0.936)
  waiting for transfers between devices: 245 us -> 212 us
    psum x1 -> x2, waiting for transfers between devices: 114 us -> 80.5 us  [the longest x1 46.1 us: one_after_other(): return lax.psum(inner, second)]
  transfers between devices with their start and end apart: 10 -> 11, of which waited for: 6 -> 7; matrix products, arithmetic and copies ran while one was open for 2% -> 2% of each run, Pallas kernels for 0% -> 0%
where the time goes in v1:
time: 455 us; the launch traced here: 446 us
  waiting for transfers between devices  212 us (47%)
  other arithmetic  75.3 us (17%)
  blocking collectives  70.4 us (15%)
  matrix products  37.6 us (8%)
  starting transfers between devices  23.9 us (5%)
  between operations  15.9 us (3%)
  local copies, waits for them, and re-layouts  10.2 us (2%)
    psum x1, waiting for transfers between devices, per_device(): lax.psum(contract(basis_rows, unscaled, 0, 1), ('sim', 'ana')) / row_count  128 us
    all_to_all x1, blocking collectives, per_device(): lax.all_to_all(outgoing, 'ana', split_axis=1, concat_axis=0, tiled=True)  53.3 us
    psum x1, waiting for transfers between devices, one_after_other(): return lax.psum(inner, second)  46.1 us
    psum x1, waiting for transfers between devices, one_after_other(): inner = lax.psum(array, first)  34.4 us
    dot_general x7, matrix products, contract(): lax.dot_general(left, right, (((left_dim,), (right_dim,)), ((), ())), pre...  34.1 us
    another operation x6, other arithmetic, per_device(): factor = jnp.linalg.cholesky(gram_matrix)  34 us
    another operation x3, other arithmetic, per_device(): jax.scipy.linalg.solve_triangular(factor, remainder, lower=True)  20.4 us
    ppermute x4, starting transfers between devices, with_halo(): before = lax.ppermute(last, axis, up)  18.6 us
  transfers between devices with their start and end apart: 11, of which 7 were waited for; matrix products, arithmetic and copies ran while one was open for 2% of the time, Pallas kernels for 0%

profile of v1, /device:TPU:0, one launch (start us, length us, event | category | flops | bytes accessed | tf_op | source)
XLA Modules:
  0.0 445.8 jit_solution(5110385182406980928)
XLA Ops:
  7.2 2.8 copy.23
  10.0 1.3 collective-permute-start
  11.4 3.3 collective-permute-start.1
  14.7 0.8 collective-permute-done.1
  15.5 1.2 select_maximum_fusion.6
  16.7 5.5 %copy_add_fusion = (f32[64,64,128]{2,0,1:T(8,128)S(1)}, f32[64,64,128]{2,0,1:T(8,128)S(1)}) fusion(f32[64,64,128]{2,1,0:T(8,128)S(1)} %copy-done.3, f32[64,64,128]{2,0,1:T(8,128)S(1)} %copy.23, f32[64,66,130]{2,0,1:T(8,128)S(1)} %select_maximum_fusion.6, f32[64,1,128]{2,0,1:T(8,128)S(1)} %collective-permute-done.1, ...), kind=kLoop, calls=%fused_computation.118 | loop fusion | flops 8912896 | bytes 14778368 | tf_op jit(solution)/shard_map/add | solution.py:61
  22.2 1.3 collective-permute-start.2
  23.5 5.3 %collective-permute-start.3 = (f32[64,1,128]{2,0,1:T(8,128)S(1)}, f32[64,1,128]{2,0,1:T(8,128)S(1)}, u32[]{:S(2)}, u32[]{:S(2)}) collective-permute-start(f32[64,1,128]{2,0,1:T(8,128)S(1)} %get-tuple-element.36), channel_id=1, source_target_pairs={{0,4},{4,8},{8,12},{12,16},{16,20},{20,24},{24,28},{1,5},{5,9},{9,... | collective-permute-start | bytes 98312 | tf_op jit(solution)/shard_map/ppermute | solution.py:25
  28.8 0.8 collective-permute-done.3
  29.6 1.2 select_maximum_fusion.4
  30.8 1.9 fusion.67
  32.8 1.3 collective-permute-start.4
  34.1 5.0 %collective-permute-start.5 = (f32[64,1,128]{2,0,1:T(8,128)S(1)}, f32[64,1,128]{2,0,1:T(8,128)S(1)}, u32[]{:S(2)}, u32[]{:S(2)}) collective-permute-start(f32[64,1,128]{2,0,1:T(8,128)S(1)} %get-tuple-element.34), channel_id=1, source_target_pairs={{0,4},{4,8},{8,12},{12,16},{16,20},{20,24},{24,28},{1,5},{5,9},{9,... | collective-permute-start | bytes 98312 | tf_op jit(solution)/shard_map/ppermute | solution.py:25
  39.1 0.8 collective-permute-done.5
  39.9 1.2 select_maximum_fusion.2
  41.1 1.8 fusion.65
  43.0 1.3 collective-permute-start.6
  44.3 5.0 %collective-permute-start.7 = (f32[64,1,128]{2,0,1:T(8,128)S(1)}, f32[64,1,128]{2,0,1:T(8,128)S(1)}, u32[]{:S(2)}, u32[]{:S(2)}) collective-permute-start(f32[64,1,128]{2,0,1:T(8,128)S(1)} %get-tuple-element.32), channel_id=1, source_target_pairs={{0,4},{4,8},{8,12},{12,16},{16,20},{20,24},{24,28},{1,5},{5,9},{9,... | collective-permute-start | bytes 98312 | tf_op jit(solution)/shard_map/ppermute | solution.py:25
  50.1 1.2 select_maximum_fusion
  51.3 3.0 multiply_reduce_fusion
  54.3 17.1 %psum.28 = f32[64]{0:T(128)S(1)} all-reduce(f32[64]{0:T(128)S(1)} %get-tuple-element.22), channel_id=1, replica_groups=mesh['sim'=8,'ana'=4] {'sim'}, use_global_device_ids=true, to_apply=%region_1.2 | all-reduce | flops 64 | bytes 512 | tf_op jit(solution)/shard_map/psum | solution.py:64
  71.5 2.0 broadcast_divide_fusion
  73.4 53.3 %all_to_all.15 = f32[64,64,128]{2,0,1:T(8,128)S(1)} all-to-all(f32[64,64,128]{2,0,1:T(8,128)S(1)} %broadcast_divide_fusion), channel_id=1, replica_groups=mesh['sim'=8,'ana'=4] {'ana'}, dimensions={1} | all-to-all | bytes 4194304 | tf_op jit(solution)/shard_map/all_to_all | solution.py:67
  126.8 1.2 copy.24
  128.0 1.0 copy-done
  129.0 5.1 %fusion.34 = f32[512,256]{0,1:T(8,128)} fusion(f32[2048,512]{1,0:T(8,128)S(1)} %bitcast.54, f32[32,8,16,128]{3,2,1,0:T(8,128)S(1)} %bitcast.55), kind=kOutput, calls=%fused_computation.71 | convolution fusion | flops 3221225472 | bytes 6815744 | tf_op jit(solution)/shard_map/dot_general | solution.py:47
  134.1 128.3 %all-reduce.9.cloned.1.call-done = f32[512,256]{0,1:T(8,128)} async-done(((f32[512,256]{0,1:T(8,128)}), f32[512,256]{0,1:T(8,128)}) %all-reduce.9.cloned.1.call-update) | async-done | bytes 524304 | tf_op jit(solution)/shard_map/psum | solution.py:69
  262.4 7.1 %convolution_subtract_fusion = f32[256,2048]{1,0:T(8,128)S(1)} fusion(f32[2048,512]{1,0:T(8,128)} %bitcast.52, f32[32,8,16,128]{3,2,1,0:T(8,128)} %bitcast.56, f32[512,256]{0,1:T(8,128)} %all-reduce.9.cloned.1.call-done), kind=kOutput, calls=%fused_computation.18 | convolution fusion | flops 3221880832 | bytes 8912896 | tf_op jit(solution)/shard_map/dot_general | solution.py:47
  269.5 2.6 fusion.75
  272.2 34.4 %all-reduce.11.cloned.1.call-done = f32[256,256]{0,1:T(8,128)} async-done(((f32[256,256]{0,1:T(8,128)}), f32[256,256]{0,1:T(8,128)}) %all-reduce.11.cloned.1.call-update) | async-done | bytes 262160 | tf_op jit(solution)/shard_map/psum | solution.py:14
  306.6 10.3 %fusion.40 = f32[2048,512]{1,0:T(8,128)} fusion(f32[2048,512]{1,0:T(8,128)} %bitcast.53, f32[768,512]{1,0:T(8,128)} %param.9), kind=kOutput, calls=%fused_computation.77 | convolution fusion | flops 6442450944 | bytes 9437184 | tf_op jit(solution)/shard_map/dot_general | solution.py:47
  316.9 46.1 %all-reduce.13.cloned.1.call-done = f32[256,256]{0,1:T(8,128)} async-done(((f32[256,256]{0,1:T(8,128)}), f32[256,256]{0,1:T(8,128)}) %all-reduce.13.cloned.1.call-update) | async-done | bytes 262160 | tf_op jit(solution)/shard_map/psum | solution.py:15
  363.0 1.0 broadcast_multiply_fusion
  364.1 1.0 fusion.47
  365.1 11.7 %cholesky.50 = f32[128,128]{1,0:T(8,128)S(1)} custom-call(f32[128,128]{1,0:T(8,128)S(1)} %cholesky.118), custom_call_target="Cholesky" | custom-call | tf_op jit(solution)/shard_map/jit(cholesky)/cholesky | solution.py:72
  376.9 9.8 %custom-call.15 = f32[1,128,128]{1,2,0:T(8,128)S(1)} custom-call(f32[1,128,128]{2,1,0:T(8,128)S(1)} %get-tuple-element.43), custom_call_target="InvertDiagBlocksLowerTriangular" | custom-call | tf_op jit(solution)/shard_map/jit(cholesky)/cholesky | solution.py:72
  387.2 11.7 %cholesky.105 = f32[128,128]{1,0:T(8,128)S(1)} custom-call(f32[128,128]{1,0:T(8,128)S(1)} %convolution_subtract_fusion.2), custom_call_target="Cholesky" | custom-call | tf_op jit(solution)/shard_map/jit(cholesky)/cholesky | solution.py:72
  401.0 1.8 fusion.42
  403.5 1.1 fusion.33
  404.6 1.0 copy.27
  405.7 4.0 while.1
  406.5 1.3 bitcast_dynamic-update-slice_fusion.2
  408.4 1.3 bitcast_dynamic-update-slice_fusion.2
  409.7 19.7 %custom-call.16 = f32[2,128,128]{1,2,0:T(8,128)S(1)} custom-call(f32[2,128,128]{2,1,0:T(8,128)S(1)} %get-tuple-element.9), custom_call_target="InvertDiagBlocksLowerTriangular" | custom-call | tf_op jit(solution)/shard_map/jit(_solve_triangular)/triangular_solve | solution.py:73
  429.4 1.1 fusion.37
  430.5 1.0 convolution_subtract_fusion.1
  431.5 1.1 fusion.55
  432.6 6.2 %convolution_add_fusion = f32[2048,512]{1,0:T(8,128)} fusion(f32[2048,512]{1,0:T(8,128)S(1)} %copy-done.1, f32[128,2048]{1,0:T(8,128)S(1)} %fusion.55, f32[128,2048]{1,0:T(8,128)S(1)} %fusion.37, f32[768,512]{1,0:T(8,128)} %param.9), kind=kOutput, calls=%fused_computation.13 | convolution fusion | flops 3222798336 | bytes 11010048 | tf_op jit(solution)/shard_map/dot_general | solution.py:47
  (49 shorter events, 4.6 us)
Async XLA Ops:
  7.2 255.3 %all-reduce.9.cloned.1.call-start = ((), (), s32[]{:S(2)}) async-start(), calls=%async_computation.1 | async-start | bytes 1048576 | tf_op jit(solution)/shard_map/psum | solution.py:69
  10.0 4.6 %collective-permute-start = (f32[64,1,128]{2,0,1:T(8,128)S(1)}, f32[64,1,128]{2,0,1:T(8,128)S(1)}, u32[]{:S(2)}, u32[]{:S(2)}) collective-permute-start(f32[64,1,128]{2,0,1:T(8,128)S(1)} %get-tuple-element.39), channel_id=1, source_target_pairs={{4,0},{8,4},{12,8},{16,12},{20,16},{24,20},{28,24},{5,1},{9,5},{13... | collective-permute-start | bytes 98312 | tf_op jit(solution)/shard_map/ppermute | solution.py:26
  11.3 5.4 %copy-start.3 = (f32[64,64,128]{2,1,0:T(8,128)S(1)}, f32[64,64,128]{2,1,0:T(8,128)}, u32[]{:S(2)}) copy-start(f32[64,64,128]{2,1,0:T(8,128)} %param.5) | copy-start | bytes 6291460
  11.3 5.4 %copy-start.5 = (f32[64,64,128]{2,1,0:T(8,128)S(1)}, f32[64,64,128]{2,1,0:T(8,128)}, u32[]{:S(2)}) copy-start(f32[64,64,128]{2,1,0:T(8,128)} %param.6) | copy-start | bytes 6291460
  11.4 5.4 %copy-start.8 = (f32[64,128]{1,0:T(8,128)S(1)}, f32[64,128]{1,0:T(8,128)}, u32[]{:S(2)}) copy-start(f32[64,128]{1,0:T(8,128)} %param.7) | copy-start | bytes 98308
  11.4 4.1 collective-permute-start.1
  22.2 6.6 %collective-permute-start.2 = (f32[64,1,128]{2,0,1:T(8,128)S(1)}, f32[64,1,128]{2,0,1:T(8,128)S(1)}, u32[]{:S(2)}, u32[]{:S(2)}) collective-permute-start(f32[64,1,128]{2,0,1:T(8,128)S(1)} %get-tuple-element.37), channel_id=1, source_target_pairs={{4,0},{8,4},{12,8},{16,12},{20,16},{24,20},{28,24},{5,1},{9,5},{13... | collective-permute-start | bytes 98312 | tf_op jit(solution)/shard_map/ppermute | solution.py:26
  23.5 6.1 %collective-permute-start.3 = (f32[64,1,128]{2,0,1:T(8,128)S(1)}, f32[64,1,128]{2,0,1:T(8,128)S(1)}, u32[]{:S(2)}, u32[]{:S(2)}) collective-permute-start(f32[64,1,128]{2,0,1:T(8,128)S(1)} %get-tuple-element.36), channel_id=1, source_target_pairs={{0,4},{4,8},{8,12},{12,16},{16,20},{20,24},{24,28},{1,5},{5,9},{9,... | collective-permute-start | bytes 98312 | tf_op jit(solution)/shard_map/ppermute | solution.py:25
  32.8 6.3 %collective-permute-start.4 = (f32[64,1,128]{2,0,1:T(8,128)S(1)}, f32[64,1,128]{2,0,1:T(8,128)S(1)}, u32[]{:S(2)}, u32[]{:S(2)}) collective-permute-start(f32[64,1,128]{2,0,1:T(8,128)S(1)} %get-tuple-element.35), channel_id=1, source_target_pairs={{4,0},{8,4},{12,8},{16,12},{20,16},{24,20},{28,24},{5,1},{9,5},{13... | collective-permute-start | bytes 98312 | tf_op jit(solution)/shard_map/ppermute | solution.py:26
  34.1 5.9 %collective-permute-start.5 = (f32[64,1,128]{2,0,1:T(8,128)S(1)}, f32[64,1,128]{2,0,1:T(8,128)S(1)}, u32[]{:S(2)}, u32[]{:S(2)}) collective-permute-start(f32[64,1,128]{2,0,1:T(8,128)S(1)} %get-tuple-element.34), channel_id=1, source_target_pairs={{0,4},{4,8},{8,12},{12,16},{16,20},{20,24},{24,28},{1,5},{5,9},{9,... | collective-permute-start | bytes 98312 | tf_op jit(solution)/shard_map/ppermute | solution.py:25
  43.0 6.3 %collective-permute-start.6 = (f32[64,1,128]{2,0,1:T(8,128)S(1)}, f32[64,1,128]{2,0,1:T(8,128)S(1)}, u32[]{:S(2)}, u32[]{:S(2)}) collective-permute-start(f32[64,1,128]{2,0,1:T(8,128)S(1)} %get-tuple-element.33), channel_id=1, source_target_pairs={{4,0},{8,4},{12,8},{16,12},{20,16},{24,20},{28,24},{5,1},{9,5},{13... | collective-permute-start | bytes 98312 | tf_op jit(solution)/shard_map/ppermute | solution.py:26
  44.3 5.9 %collective-permute-start.7 = (f32[64,1,128]{2,0,1:T(8,128)S(1)}, f32[64,1,128]{2,0,1:T(8,128)S(1)}, u32[]{:S(2)}, u32[]{:S(2)}) collective-permute-start(f32[64,1,128]{2,0,1:T(8,128)S(1)} %get-tuple-element.32), channel_id=1, source_target_pairs={{0,4},{4,8},{8,12},{12,16},{16,20},{20,24},{24,28},{1,5},{5,9},{9,... | collective-permute-start | bytes 98312 | tf_op jit(solution)/shard_map/ppermute | solution.py:25
  126.7 2.2 copy-start
  128.0 6.1 %copy-start.2 = (f32[64,4,16,128]{3,2,0,1:T(8,128)}, f32[64,4,16,128]{3,2,0,1:T(8,128)S(1)}, u32[]{:S(2)}) copy-start(f32[64,4,16,128]{3,2,0,1:T(8,128)S(1)} %copy.24) | copy-start | bytes 6291460
  134.1 172.5 %all-reduce.11.cloned.1.call-start = ((), (), s32[]{:S(2)}) async-start(), calls=%async_computation.2 | async-start | bytes 524288 | tf_op jit(solution)/shard_map/psum | solution.py:14
  272.1 90.8 %all-reduce.13.cloned.1.call-start = ((), (), s32[]{:S(2)}) async-start(), calls=%async_computation.3 | async-start | bytes 524288 | tf_op jit(solution)/shard_map/psum | solution.py:15
  363.9 39.6 %copy-start.6 = (f32[512,256]{0,1:T(8,128)S(1)}, f32[512,256]{0,1:T(8,128)}, u32[]{:S(2)}) copy-start(f32[512,256]{0,1:T(8,128)} %all-reduce.9.cloned.1.call-done) | copy-start | bytes 1572868
  401.0 2.6 copy-start.4
  403.5 2.1 copy-start.7
  430.4 2.2 copy-start.1
Sparse Core Ops, SparseCore 0:
  134.2 128.2 all-reduce.8
  272.2 34.3 all-reduce.10
  309.6 53.2 all-reduce.12
